TPU v7x, 256 devices: a whole 4x4x8 slice. The times are simulated.
256 devices in a mesh: stack: 4 (over y), tile: 64 (over z, x, core).
Axes of the slice: x: 4, y: 4, z: 8, core: 2. Of those that a mesh axis runs over, the one named last changes fastest.
Arguments:
- displacement: float32 [32, 2, 512, 128], P('stack', None, 'tile'), may hold values from -6 to 6
- lens_coef: float32 [32, 2, 8], P('stack'), may hold values from -1.8 to 1.8
- stiff_class: int32 [32, 512, 128], P('stack', 'tile'), may hold values from 0 to 3
- stiff_table: float32 [4], replicated, may hold values from 0.5 to 2
- match_src: int32 [262144], P(('stack', 'tile')), may hold values from 0 to 8191
- match_owner: int32 [262144, 1], P(('stack', 'tile')), may hold values from 0 to 63; in each aligned block of 1024 rows (0 to 1023, 1024 to 2047, ...) at most 24 rows name the same one
- match_dst: int32 [262144], P(('stack', 'tile')), may hold values from 0 to 1023
- match_level: int32 [262144], P(('stack', 'tile')), may hold values from 0 to 8
- match_offset: float32 [2, 262144], P(None, ('stack', 'tile')), may hold values from -6 to 6
Outputs:
- relaxed: float32 [32, 2, 512, 128], P('stack', None, 'tile')
- lens_fit: float32 [32, 2, 8], P('stack')
Inputs may be any that keep to these rules, and one draw needn't show every extreme that they name: `match_owner`: among the 1024 entries of one device's list no tile index is named more than 24 times, a bound that some block reaches. `match_level`: level 0 marks a padding entry, whose match carries no force.
All inputs are finite; a program needn't handle non-finite values.
Results may differ from a plain program's by a relative error of at most 0.0003.
Values sent between devices are 32-bit elements; how exact they have to be, the bound alone decides.
A program may use at most 64 MiB of HBM per device.

v0:
```python
import functools

import jax
import jax.numpy as jnp
import numpy as np
from jax import lax
from jax.experimental import pallas as pl
from jax.experimental.pallas import tpu as pltpu
from jax.sharding import PartitionSpec as P

ITERS = 4
STEP_RATE = 0.04
LENS_RATE = 4.0
MESH = pl.DeviceIdType.MESH
F32, BF16, I32 = jnp.float32, jnp.bfloat16, jnp.int32

SEC, EXT = 8, 9
TILES, STACKS = 64, 4
HALF = 12
GROW = 48
LENS = 8

NEAR = [(dx, dc) for dx in (2, 1, 3, 0) for dc in (1, 0)]
STEPS = [(dr, dc, 1.0 if dr == 0 or dc == 0 else 0.5) for dr in (-1, 0, 1) for dc in (-1, 0, 1) if dr or dc]


def iota(shape, dim):
    return lax.broadcasted_iota(I32, shape, dim)


def split(x):
    high = x.astype(BF16).astype(F32)
    return high, x - high


def rowpos(side, comp, i):
    return side * 24 + (comp * 8 + i if i < 8 else 16 + comp * 4 + i - 8)


def fold(x):
    for step in (8, 16, 32, 64):
        x = x + pltpu.roll(x, step, 1)
    return x


def pack_rows(a, b):
    last = jnp.where(iota((8, 128), 0) < 4, a[8:16], pltpu.roll(b[8:16], 4, 0))
    return jnp.concatenate([a[0:8], b[0:8], last], axis=0)


def kernel(
    disp, lens, scls, stab, msrc, mown, mdst, mlev, moff,
    dout, cout,
    D, K, W, WS, S, F, msg, box, CH, Q, rowix, offs, base, pos, tin, pull, lval, C, G, tmp, wrow,
    hs, hr, khs, khr, ys, yr, cy,
    a_send, a_recv, h_send, h_recv, k_send, k_recv, y_send, y_recv, s_send, s_recv,
):
    t = lax.axis_index("tile")
    g = lax.axis_index("stack")
    z, a = lax.div(t, 8), lax.rem(t, 8)
    x, c = lax.div(a, 2), lax.rem(a, 2)
    up_g, down_g = lax.rem(g + 1, STACKS), lax.rem(g + STACKS - 1, STACKS)
    up_t, down_t = lax.rem(t + 1, TILES), lax.rem(t + TILES - 1, TILES)

    def peer(dz, dx, dc):
        pz, px, pc = lax.rem(z + dz, 8), lax.rem(x + dx, 4), lax.rem(c + dc, 2)
        return pz * 8 + px * 2 + pc

    def each_peer(do):
        def along_z(k, carry):
            odd = lax.rem(k, 2)
            dz = 4 + lax.div(k, 2) - odd * (k)
            for dx, dc in NEAR:
                do(peer(dz, dx, dc))
            return carry

        lax.fori_loop(0, 7, along_z, 0)
        for dx, dc in NEAR:
            if dx or dc:
                do(peer(0, dx, dc))

    barrier = pltpu.get_barrier_semaphore()

    def greet(p):
        pl.semaphore_signal(barrier, inc=1, device_id={"tile": p}, device_id_type=MESH)

    each_peer(greet)
    for other in (up_g, down_g):
        pl.semaphore_signal(barrier, inc=1, device_id={"stack": other}, device_id_type=MESH)

    def send_rows(par):
        def one(p):
            pltpu.make_async_remote_copy(
                src_ref=msg.at[p], dst_ref=box.at[par, t], send_sem=a_send, recv_sem=a_recv.at[par],
                device_id={"tile": p}, device_id_type=MESH,
            ).start()

        each_peer(one)
        box[par, t] = msg[t]

    def wait_rows(par):
        got = box.at[par, pl.ds(0, TILES - 1)]
        pltpu.make_async_copy(got, got, a_recv.at[par]).wait()
        sent = msg.at[pl.ds(0, TILES - 1)]
        pltpu.make_async_copy(sent, sent, a_send).wait()

    def y_copy(src, dst, sems, recv, index, other):
        return pltpu.make_async_remote_copy(
            src_ref=src, dst_ref=dst, send_sem=sems.at[index], recv_sem=recv.at[index],
            device_id={"stack": other}, device_id_type=MESH,
        )

    def t_copy(src, dst, send, recv, other):
        return pltpu.make_async_remote_copy(
            src_ref=src, dst_ref=dst, send_sem=send, recv_sem=recv,
            device_id={"tile": other}, device_id_type=MESH,
        )

    lane8 = iota((8, 128), 1)
    sub8 = iota((8, 128), 0)
    group8 = lax.shift_right_logical(lane8, 3) - GROW // 8
    own_group = group8 == sub8

    D[0:SEC] = disp[...]
    cls = scls[...]
    stiff = jnp.zeros(cls.shape, F32)
    for k in range(4):
        stiff = jnp.where(cls == k, stab[k], stiff)
    K[0:SEC] = stiff
    C[...] = jnp.zeros_like(C)
    tmp[...] = jnp.zeros_like(tmp)
    for comp in range(2):
        tmp[:, 0:LENS] = lens[:, comp, :]
        wide = fold(tmp[...])
        C[comp : comp + 1] = jnp.sum(jnp.where(own_group, wide, 0.0), axis=0, keepdims=True)

    own = mown[...]
    tri_r, tri_c = iota((128, 256), 0), iota((128, 256), 1)
    tri = jnp.where(tri_r <= tri_c, 1.0, 0.0).astype(BF16)
    lane_own = iota((TILES, 128), 0)
    before = jnp.zeros((TILES, 128), F32)
    src, dst, lev = msrc[...], mdst[...], mlev[...]
    srow, scol = lax.shift_right_logical(src, 7), src & 127
    drow, dcol = lax.shift_right_logical(dst, 7), dst & 127
    live = jnp.where(srow + g * 64 >= STACKS * 64 - 8, 0, lev)
    ints = [v.astype(F32) for v in (srow, scol, drow, dcol, live)]
    slots = jnp.zeros((11 * 16, 128), F32)
    for j in range(8):
        own_j = own[j : j + 1]
        hot = jnp.where(lane_own == own_j, 1.0, 0.0)
        counted = jnp.dot(hot.astype(BF16), tri, preferred_element_type=F32)
        rank = jnp.sum(hot * (counted[:, :128] + before), axis=0, keepdims=True) - 1.0
        before = before + counted[:, 128:]
        rank = rank.astype(I32)
        high = jnp.where(rank >= HALF, 1, 0)
        row_hot = iota((16, 128), 0) == rank - HALF * high
        slot_hot = jnp.where(iota((128, 128), 0) == own_j + TILES * high, 1.0, 0.0).astype(BF16)
        values = [v[j : j + 1] for v in ints]
        for comp in range(2):
            off = moff[comp : comp + 1, j * 128 : (j + 1) * 128]
            first, rest = split(off)
            second, third = split(rest)
            values += [first, second, third]
        picked = jnp.concatenate([jnp.where(row_hot, v, 0.0) for v in values], axis=0).astype(BF16)
        slots = slots + lax.dot_general(picked, slot_hot, (((1,), (1,)), ((), ())), preferred_element_type=F32)
    sl = [slots[16 * v : 16 * v + 16] for v in range(11)]
    mine = sl[0:5] + [sl[5] + sl[6] + sl[7], sl[8] + sl[9] + sl[10]]

    tin[...] = jnp.zeros_like(tin)
    tin[0:112] = jnp.concatenate(mine, axis=0)
    turned = tin[...].T
    msg[:, 0, :] = turned[0:TILES]
    msg[:, 1, :] = turned[TILES:]

    pl.semaphore_wait(barrier, TILES - 1 + 2)
    first = [
        y_copy(D.at[0], D.at[SEC], s_send, s_recv, 0, down_g),
        y_copy(K.at[0], K.at[SEC], s_send, s_recv, 1, down_g),
        y_copy(C, cy, s_send, s_recv, 2, down_g),
    ]
    for copy in first:
        copy.start()
    send_rows(0)

    peer_row = (iota((16, 128), 1) & (TILES - 1)) * 8
    own_row0 = t * 8

    def side_tables(side, values):
        sr, sc, dr, dc, level = [v.astype(I32) for v in values[0:5]]
        ox, oy = values[5], values[6]
        sign = 1.0 if side == 0 else -1.0
        s_in, sec = sr & 7, lax.shift_right_logical(sr, 3)
        ysrc = (own_row0 if side == 0 else peer_row) + s_in
        ydst = (peer_row if side == 0 else own_row0) + dr
        ramp_s = (1.0 + ysrc.astype(F32) * (2.0 / 512)) * sign
        ramp_d = (1.0 + ydst.astype(F32) * (2.0 / 512)) * -sign
        offs[24 * side : 24 * side + 24] = pack_rows(ox, oy) * sign
        weight = values[4] * 0.125
        base[24 * side : 24 * side + 24] = pack_rows(weight, weight)
        rowix[side, 0] = sr if side == 0 else sec * 8 + 8 + dr
        rowix[side, 1] = sec
        own_col = sc if side == 0 else dc
        for i in range(HALF):
            at = slice(i * 128, (i + 1) * 128)
            CH[side, :, at] = jnp.where(iota((128, 128), 0) == own_col[i : i + 1], 1.0, 0.0).astype(BF16)
            parts = []
            for col, ramp in ((sc, ramp_s), (dc, ramp_d)):
                turn = (sub8 * col[i : i + 1]) & 255
                high, low = split(jnp.cos(turn.astype(F32) * (np.pi / 128)) * ramp[i : i + 1])
                parts += [high, high, low]
            Q[side, :, at] = jnp.concatenate(parts, axis=0).astype(BF16)

    side_tables(0, mine)
    cos_k = (lane8 - GROW) & 7
    col128 = iota((128, 128), 0)
    k128 = (iota((128, 128), 1) - GROW) & 7
    turn = (col128 * k128) & 255
    cos_hi, cos_lo = split(jnp.cos(turn.astype(F32) * (np.pi / 128)))
    cos_cat = jnp.concatenate([cos_hi, cos_hi, cos_lo], axis=0).astype(BF16)

    for copy in first:
        copy.wait()
    for comp in range(2):
        C[comp : comp + 1] = C[comp : comp + 1] + jnp.where(
            group8[0:1] == SEC, pltpu.roll(cy[comp : comp + 1], LENS * SEC, 1), 0.0
        )
    hs[...] = jnp.zeros_like(hs)
    khs[...] = jnp.zeros_like(khs)

    def beside(par):
        return [
            t_copy(hs.at[par, 0], hr.at[par, 1], h_send.at[par, 0], h_recv.at[par, 1], down_t),
            t_copy(hs.at[par, 1], hr.at[par, 0], h_send.at[par, 1], h_recv.at[par, 0], up_t),
        ]

    def send_beside(par):
        for s in range(EXT):
            for comp in range(2):
                r = s * 2 + comp
                hs[par, 0, r : r + 1] = D[s, comp, 0:1]
                hs[par, 1, r : r + 1] = D[s, comp, 7:8]
        for copy in beside(par):
            copy.start()

    for s in range(EXT):
        khs[0, s : s + 1] = K[s, 0:1]
        khs[1, s : s + 1] = K[s, 7:8]
    kcopies = [
        t_copy(khs.at[0], khr.at[1], k_send.at[0], k_recv.at[1], down_t),
        t_copy(khs.at[1], khr.at[0], k_send.at[1], k_recv.at[0], up_t),
    ]
    for copy in kcopies:
        copy.start()
    send_beside(0)

    def shifted(v, low, high):
        above = jnp.where(sub8 == 0, low, pltpu.roll(v, 1, 0))
        below = jnp.where(sub8 == 7, high, pltpu.roll(v, 7, 0))
        for dr, row in ((-1, above), (0, v), (1, below)):
            for dc in (-1, 0, 1):
                if dr or dc:
                    yield row if dc == 0 else pltpu.roll(row, 1 if dc < 0 else 127, 1)

    for copy in kcopies:
        copy.wait()
    has_low, has_high = jnp.where(t > 0, 1.0, 0.0), jnp.where(t < TILES - 1, 1.0, 0.0)
    for s in range(EXT):
        v = K[s]
        total = jnp.zeros((8, 128), F32)
        near = shifted(v, khr[0, s : s + 1] * has_low, khr[1, s : s + 1] * has_high)
        for n, ((dr, dc, scale), other) in enumerate(zip(STEPS, near)):
            w = scale * jnp.minimum(v, other)
            if dc:
                w = jnp.where(lane8 == (0 if dc < 0 else 127), 0.0, w)
            W[n, s] = w
            total = total + w
        WS[s] = total

    def turn_rows(par):
        both = jnp.concatenate([box[par, :, 0, :], box[par, :, 1, :]], axis=0)
        return both, both.T

    wait_rows(0)
    _, theirs = turn_rows(0)
    side_tables(1, [theirs[16 * v : 16 * v + 16] for v in range(7)])
    tin[...] = jnp.zeros_like(tin)
    G[...] = jnp.zeros_like(G)
    wrow[...] = jnp.zeros_like(wrow)

    ramp8 = 1.0 + (own_row0 + sub8).astype(F32) * (2.0 / 512)
    lens_step = LENS_RATE * SEC / (1024 * TILES)

    def gather():
        d_hi, d_lo = split(D[...].reshape(EXT * 16, 128))
        both = jnp.concatenate([d_hi, d_lo], axis=1).astype(BF16)
        for side in range(2):
            for n in range(HALF // 2):
                hot = CH[side, :, n * 256 : (n + 1) * 256]
                got = jnp.dot(both, jnp.concatenate([hot, hot], axis=0), preferred_element_type=F32)
                for m in range(2):
                    i = 2 * n + m
                    row = rowix[side, 0, i : i + 1]
                    sec, within = lax.shift_right_logical(row, 3), row & 7
                    at = slice(m * 128, (m + 1) * 128)
                    total = [jnp.zeros((8, 128), F32), jnp.zeros((8, 128), F32)]
                    for s in range(EXT):
                        hit = sec == s
                        for comp in range(2):
                            r = (s * 2 + comp) * 8
                            total[comp] = jnp.where(hit, got[r : r + 8, at], total[comp])
                    for comp in range(2):
                        value = jnp.sum(jnp.where(sub8 == within, total[comp], 0.0), axis=0, keepdims=True)
                        r = rowpos(side, comp, i)
                        tin[r : r + 1] = value

    def exchange(par):
        turned = tin[...].T
        for comp in range(2):
            msg[:, comp, :] = turned[comp * TILES : (comp + 1) * TILES] + G[comp : comp + 1]
        send_rows(par)

    def take_gradient(both):
        for comp in range(2):
            total = jnp.sum(both[comp * TILES : (comp + 1) * TILES], axis=0, keepdims=True)
            C[comp : comp + 1] = C[comp : comp + 1] + lens_step * jnp.where(group8[0:1] >= 0, total, 0.0)

    def lens_values():
        rows = []
        for comp in range(2):
            wide = jnp.broadcast_to(C[comp : comp + 1], (8, 128))
            s_hi, s_lo = split(fold(jnp.where(own_group, wide, 0.0)))
            d_hi, d_lo = split(fold(jnp.where(group8 == sub8 + 1, wide, 0.0)))
            block = lax.shift_right_logical(lane8, 3)
            row = jnp.where(block == 1, s_lo, s_hi)
            row = jnp.where(block >= 3, d_hi, row)
            rows.append(jnp.where(block == 4, d_lo, row))
        coef = jnp.concatenate(rows, axis=0)[:, 0:48].astype(BF16)
        for side in range(2):
            for n in range(HALF // 2):
                got = jnp.dot(coef, Q[side, :, n * 256 : (n + 1) * 256], preferred_element_type=F32)
                for m in range(2):
                    i = 2 * n + m
                    hit = rowix[side, 1, i : i + 1] == sub8
                    for comp in range(2):
                        r = rowpos(side, comp, i)
                        lval[r : r + 1] = jnp.sum(
                            jnp.where(hit, got[comp * 8 : comp * 8 + 8, m * 128 : (m + 1) * 128], 0.0),
                            axis=0, keepdims=True,
                        )

    def forces(theirs):
        other = jnp.concatenate([theirs[24:48], theirs[0:24]], axis=0)
        r = tin[0:48] - other + offs[...] + lval[...]
        sq = r * r
        for side in range(2):
            b = side * 24
            near = sq[b : b + 8] + sq[b + 8 : b + 16]
            last = sq[b + 16 : b + 24]
            last = last + pltpu.roll(last, 4, 0)
            size = jnp.concatenate([near, near, last], axis=0)
            pull[b : b + 24] = -base[b : b + 24] * r[b : b + 24] / (1.0 + size * 0.25)

    def scatter():
        rows72 = iota((EXT * 8, 128), 0)
        total = jnp.zeros((4 * EXT * 8, 128), F32)
        for side in range(2):
            for n in range(HALF // 2):
                cols = []
                for m in range(2):
                    i = 2 * n + m
                    hit = rows72 == rowix[side, 0, i : i + 1]
                    pieces = []
                    for comp in range(2):
                        r = rowpos(side, comp, i)
                        pieces += list(split(pull[r : r + 1]))
                    cols.append(jnp.concatenate([jnp.where(hit, p, 0.0) for p in pieces], axis=0))
                spread = jnp.concatenate(cols, axis=1).astype(BF16)
                total = total + lax.dot_general(
                    spread, CH[side, :, n * 256 : (n + 1) * 256], (((1,), (1,)), ((), ())),
                    preferred_element_type=F32,
                )
        for comp in range(2):
            b = comp * 2 * EXT * 8
            F[:, comp] = (total[b : b + EXT * 8] + total[b + EXT * 8 : b + 2 * EXT * 8]).reshape(EXT, 8, 128)

    def springs(par):
        for s in range(EXT):
            for comp in range(2):
                r = s * 2 + comp
                v = D[s, comp]
                total = -WS[s] * v
                near = shifted(v, hr[par, 0, r : r + 1], hr[par, 1, r : r + 1])
                for n, other in enumerate(near):
                    total = total + W[n, s] * other
                S[s, comp] = total

    def gradient():
        for s in range(EXT):
            for comp in range(2):
                r = comp * 16 + s
                wrow[r : r + 1] = jnp.sum(ramp8 * F[s, comp], axis=0, keepdims=True)
        w_hi, w_lo = split(wrow[...])
        cat = jnp.concatenate([w_hi, w_lo, w_hi], axis=1).astype(BF16)
        out = jnp.dot(cat, cos_cat, preferred_element_type=F32)
        group16 = lax.shift_right_logical(iota((16, 128), 1), 3) - GROW // 8
        mask = (group16 == iota((16, 128), 0)) & (group16 < EXT)
        for comp in range(2):
            G[comp : comp + 1] = jnp.sum(
                jnp.where(mask, out[comp * 16 : comp * 16 + 16], 0.0), axis=0, keepdims=True
            )

    def sweep(it, carry):
        par = lax.rem(it + 1, 2)
        hpar = lax.rem(it, 2)
        gather()
        exchange(par)
        for copy in beside(hpar):
            copy.wait()
        springs(hpar)
        wait_rows(par)
        both, theirs = turn_rows(par)
        take_gradient(both)
        lens_values()
        forces(theirs)
        scatter()
        ys[hpar, 0] = F[SEC]
        ys[hpar, 1] = F[0]
        copies = [
            t_like(hpar, 0, up_g),
            t_like(hpar, 1, down_g),
        ]
        for copy in copies:
            copy.start()
        for copy in copies:
            copy.wait()
        F[0] = F[0] + yr[hpar, 0]
        F[SEC] = F[SEC] + yr[hpar, 1]
        gradient()
        D[...] = D[...] + STEP_RATE * (S[...] + F[...])
        send_beside(1 - hpar)
        return carry

    def t_like(par, way, other):
        return pltpu.make_async_remote_copy(
            src_ref=ys.at[par, way], dst_ref=yr.at[par, way], send_sem=y_send.at[par, way],
            recv_sem=y_recv.at[par, way], device_id={"stack": other}, device_id_type=MESH,
        )

    lax.fori_loop(0, ITERS, sweep, 0)
    dout[...] = D[0:SEC]
    last = (ITERS + 1) % 2
    exchange(last)
    for copy in beside(ITERS % 2):
        copy.wait()
    wait_rows(last)
    both = jnp.concatenate([box[last, :, 0, :], box[last, :, 1, :]], axis=0)
    take_gradient(both)
    for comp in range(2):
        wide = fold(jnp.where(own_group, jnp.broadcast_to(C[comp : comp + 1], (8, 128)), 0.0))
        cout[:, comp, :] = wide[:, 0:LENS]


def on_device(displacement, lens_coef, stiff_class, stiff_table, match_src, match_owner, match_dst, match_level, match_offset):
    vmem = pl.BlockSpec(memory_space=pltpu.VMEM)
    smem = pl.BlockSpec(memory_space=pltpu.SMEM)
    V, DMA = pltpu.VMEM, pltpu.SemaphoreType.DMA
    lists = [a.reshape(8, 128) for a in (match_src, match_owner, match_dst, match_level)]
    scratch = [
        V((EXT, 2, 8, 128), F32),
        V((EXT, 8, 128), F32),
        V((8, EXT, 8, 128), F32),
        V((EXT, 8, 128), F32),
        V((EXT, 2, 8, 128), F32),
        V((EXT, 2, 8, 128), F32),
        V((TILES, 2, 128), F32),
        V((2, TILES, 2, 128), F32),
        V((2, 128, HALF * 128), BF16),
        V((2, 48, HALF * 128), BF16),
        V((2, 2, 16, 128), I32),
        V((48, 128), F32),
        V((48, 128), F32),
        V((48, 128), F32),
        V((128, 128), F32),
        V((48, 128), F32),
        V((48, 128), F32),
        V((8, 128), F32),
        V((8, 128), F32),
        V((8, 128), F32),
        V((32, 128), F32),
        V((2, 2, 24, 128), F32),
        V((2, 2, 24, 128), F32),
        V((2, 16, 128), F32),
        V((2, 16, 128), F32),
        V((2, 2, 2, 8, 128), F32),
        V((2, 2, 2, 8, 128), F32),
        V((8, 128), F32),
        DMA, DMA((2,)), DMA((2, 2)), DMA((2, 2)), DMA((2,)), DMA((2,)), DMA((2, 2)), DMA((2, 2)), DMA((3,)), DMA((3,)),
    ]
    return pl.pallas_call(
        kernel,
        out_shape=(
            jax.ShapeDtypeStruct((SEC, 2, 8, 128), F32),
            jax.ShapeDtypeStruct((SEC, 2, LENS), F32),
        ),
        in_specs=[vmem, vmem, vmem, smem] + [vmem] * 5,
        out_specs=(vmem, vmem),
        scratch_shapes=scratch,
        compiler_params=pltpu.CompilerParams(
            collective_id=0, has_side_effects=True, vmem_limit_bytes=32 * 1024 * 1024
        ),
        name="relax",
    )(displacement, lens_coef, stiff_class, stiff_table, *lists, match_offset)


def solution(mesh):
    in_specs = (
        P("stack", None, "tile", None),
        P("stack", None, None),
        P("stack", "tile", None),
        P(),
        P(("stack", "tile")),
        P(("stack", "tile"), None),
        P(("stack", "tile")),
        P(("stack", "tile")),
        P(None, ("stack", "tile")),
    )
    out_specs = (P("stack", None, "tile", None), P("stack", None, None))
    return jax.shard_map(on_device, mesh=mesh, in_specs=in_specs, out_specs=out_specs, check_vma=False)
```

profile of v0, /device:TPU:1, one launch (start us, length us, event | category | flops | bytes accessed | tf_op | source)
XLA Modules:
  0.0 75.8 jit_solution(18345029079561427709)
XLA Ops:
  0.6 0.0 copy-start.4
  0.6 0.0 copy-start.8
  0.7 0.7 copy-done.4
  1.3 0.0 copy-done.8
  1.3 0.0 copy-start
  1.3 0.8 %copy-done = f32[8,2,8,128]{3,2,1,0:T(8,128)S(1)} copy-done((f32[8,2,8,128]{3,2,1,0:T(8,128)S(1)}, f32[8,2,8,128]{3,2,1,0:T(8,128)}, u32[]{:S(2)}) %copy-start) | copy-done | bytes 65560
  2.2 0.0 copy-start.1
  2.2 0.8 copy-done.1
  2.9 0.0 copy-start.2
  2.9 0.7 copy-done.2
  3.6 0.0 copy-start.3
  3.6 0.7 copy-done.3
  4.3 0.0 copy-start.5
  4.3 0.7 copy-done.5
  5.0 0.0 copy-start.6
  5.0 0.7 copy-done.6
  5.7 0.0 copy-start.7
  5.7 0.7 copy-done.7
  6.4 68.2 %relax.1 = (f32[8,2,8,128]{3,2,1,0:T(8,128)S(1)}, f32[8,2,8]{2,1,0:T(2,128)S(1)}) custom-call(f32[8,2,8,128]{3,2,1,0:T(8,128)S(1)} %copy-done, f32[8,2,8]{2,1,0:T(2,128)S(1)} %copy-done.2, s32[8,8,128]{2,1,0:T(8,128)S(1)} %copy-done.1, f32[4]{0:T(128)S(1)} %copy-done.8, s32[8,128]{1,0:T(8,128)S(1)} %bitcast.4, s32[8,128]{1,0:T(8,128)S(1)} %bitcast.5, ...), custom_call_target="tpu_custom_call" | custom-call | tf_op jit(solution)/shard_map/relax/pallas_call | solution.py:499
  74.6 0.6 copy.13
  75.2 0.6 copy.14
Async XLA Ops:
  0.6 0.7 copy-start.4
  0.6 0.7 copy-start.8
  1.3 0.8 %copy-start = (f32[8,2,8,128]{3,2,1,0:T(8,128)S(1)}, f32[8,2,8,128]{3,2,1,0:T(8,128)}, u32[]{:S(2)}) copy-start(f32[8,2,8,128]{3,2,1,0:T(8,128)} %disp.1) | copy-start | bytes 196612
  2.2 0.8 copy-start.1
  2.9 0.7 copy-start.2
  3.6 0.7 copy-start.3
  4.3 0.7 copy-start.5
  5.0 0.7 copy-start.6
  5.7 0.7 copy-start.7
where the time goes:
time: 76.2 us; the launch traced here: 75.8 us
  Pallas kernels  68.2 us (90%)
  local copies, waits for them, and re-layouts  6.95 us (9%)
    pallas_call x1, Pallas kernels, on_device(): pl.pallas_call(kernel, out_shape=(jax.ShapeDtypeStruct((SEC, 2, 8, 128),...  68.2 us
    unnamed x20, local copies, waits for them, and re-layouts  6.95 us

commit v1 on v0

--- a/solution.py
+++ b/solution.py
@@ -49,11 +49,12 @@
 
 
 def kernel(
-    disp, lens, scls, stab, msrc, mown, mdst, mlev, moff,
+    disp_in, lens_in, scls_in, stab_in, msrc_in, mown_in, mdst_in, mlev_in, moff_in,
     dout, cout,
-    D, K, W, WS, S, F, msg, box, CH, Q, rowix, offs, base, pos, tin, pull, lval, C, G, tmp, wrow,
+    lens, scls, stab, msrc, mown, mdst, mlev, moff,
+    D, K, W, WS, S, F, msg, box, CH, Q, rowix, offs, base, tin, pull, lval, C, G, tmp, wrow,
     hs, hr, khs, khr, ys, yr, cy,
-    a_send, a_recv, h_send, h_recv, k_send, k_recv, y_send, y_recv, s_send, s_recv,
+    in_sem, a_send, a_recv, h_send, h_recv, k_send, k_recv, y_send, y_recv, s_send, s_recv,
 ):
     t = lax.axis_index("tile")
     g = lax.axis_index("stack")
@@ -79,6 +80,15 @@
             if dx or dc:
                 do(peer(0, dx, dc))
 
+    loads = [
+        pltpu.make_async_copy(src, dst, in_sem.at[n])
+        for n, (src, dst) in enumerate((
+            (mown_in, mown), (msrc_in, msrc), (mdst_in, mdst), (mlev_in, mlev), (moff_in, moff),
+            (disp_in, D.at[pl.ds(0, SEC)]), (scls_in, scls), (lens_in, lens), (stab_in, stab),
+        ))
+    ]
+    for copy in loads:
+        copy.start()
     barrier = pltpu.get_barrier_semaphore()
 
     def greet(p):
@@ -121,19 +131,8 @@
     group8 = lax.shift_right_logical(lane8, 3) - GROW // 8
     own_group = group8 == sub8
 
-    D[0:SEC] = disp[...]
-    cls = scls[...]
-    stiff = jnp.zeros(cls.shape, F32)
-    for k in range(4):
-        stiff = jnp.where(cls == k, stab[k], stiff)
-    K[0:SEC] = stiff
-    C[...] = jnp.zeros_like(C)
-    tmp[...] = jnp.zeros_like(tmp)
-    for comp in range(2):
-        tmp[:, 0:LENS] = lens[:, comp, :]
-        wide = fold(tmp[...])
-        C[comp : comp + 1] = jnp.sum(jnp.where(own_group, wide, 0.0), axis=0, keepdims=True)
-
+    for copy in loads[0:5]:
+        copy.wait()
     own = mown[...]
     tri_r, tri_c = iota((128, 256), 0), iota((128, 256), 1)
     tri = jnp.where(tri_r <= tri_c, 1.0, 0.0).astype(BF16)
@@ -173,6 +172,22 @@
     msg[:, 1, :] = turned[TILES:]
 
     pl.semaphore_wait(barrier, TILES - 1 + 2)
+    send_rows(0)
+
+    for copy in loads[5:]:
+        copy.wait()
+    cls = scls[...]
+    stiff = jnp.zeros(cls.shape, F32)
+    for k in range(4):
+        stiff = jnp.where(cls == k, stab[k], stiff)
+    K[0:SEC] = stiff
+    C[...] = jnp.zeros_like(C)
+    tmp[...] = jnp.zeros_like(tmp)
+    for comp in range(2):
+        tmp[:, 0:LENS] = lens[:, comp, :]
+        wide = fold(tmp[...])
+        C[comp : comp + 1] = jnp.sum(jnp.where(own_group, wide, 0.0), axis=0, keepdims=True)
+
     first = [
         y_copy(D.at[0], D.at[SEC], s_send, s_recv, 0, down_g),
         y_copy(K.at[0], K.at[SEC], s_send, s_recv, 1, down_g),
@@ -180,16 +195,25 @@
     ]
     for copy in first:
         copy.start()
-    send_rows(0)
 
     peer_row = (iota((16, 128), 1) & (TILES - 1)) * 8
     own_row0 = t * 8
 
-    def side_tables(side, values):
-        sr, sc, dr, dc, level = [v.astype(I32) for v in values[0:5]]
+    def node_tables(side, values):
+        sr, sc, dr, dc = [v.astype(I32) for v in values[0:4]]
+        sec = lax.shift_right_logical(sr, 3)
+        rowix[side, 0] = sr if side == 0 else sec * 8 + 8 + dr
+        rowix[side, 1] = sec
+        own_col = sc if side == 0 else dc
+        for i in range(HALF):
+            at = slice(i * 128, (i + 1) * 128)
+            CH[side, :, at] = jnp.where(iota((128, 128), 0) == own_col[i : i + 1], 1.0, 0.0).astype(BF16)
+
+    def pull_tables(side, values):
+        sr, sc, dr, dc = [v.astype(I32) for v in values[0:4]]
         ox, oy = values[5], values[6]
         sign = 1.0 if side == 0 else -1.0
-        s_in, sec = sr & 7, lax.shift_right_logical(sr, 3)
+        s_in = sr & 7
         ysrc = (own_row0 if side == 0 else peer_row) + s_in
         ydst = (peer_row if side == 0 else own_row0) + dr
         ramp_s = (1.0 + ysrc.astype(F32) * (2.0 / 512)) * sign
@@ -197,12 +221,8 @@
         offs[24 * side : 24 * side + 24] = pack_rows(ox, oy) * sign
         weight = values[4] * 0.125
         base[24 * side : 24 * side + 24] = pack_rows(weight, weight)
-        rowix[side, 0] = sr if side == 0 else sec * 8 + 8 + dr
-        rowix[side, 1] = sec
-        own_col = sc if side == 0 else dc
         for i in range(HALF):
             at = slice(i * 128, (i + 1) * 128)
-            CH[side, :, at] = jnp.where(iota((128, 128), 0) == own_col[i : i + 1], 1.0, 0.0).astype(BF16)
             parts = []
             for col, ramp in ((sc, ramp_s), (dc, ramp_d)):
                 turn = (sub8 * col[i : i + 1]) & 255
@@ -210,7 +230,39 @@
                 parts += [high, high, low]
             Q[side, :, at] = jnp.concatenate(parts, axis=0).astype(BF16)
 
-    side_tables(0, mine)
+    def gather(side):
+        d_hi, d_lo = split(D[side : side + SEC].reshape(SEC * 16, 128))
+        both = jnp.concatenate([d_hi, d_lo], axis=1).astype(BF16)
+        for _ in range(1):
+            for n in range(HALF // 2):
+                hot = CH[side, :, n * 256 : (n + 1) * 256]
+                got = jnp.dot(both, jnp.concatenate([hot, hot], axis=0), preferred_element_type=F32)
+                for m in range(2):
+                    i = 2 * n + m
+                    row = rowix[side, 0, i : i + 1]
+                    sec, within = lax.shift_right_logical(row, 3), row & 7
+                    at = slice(m * 128, (m + 1) * 128)
+                    total = [jnp.zeros((8, 128), F32), jnp.zeros((8, 128), F32)]
+                    for s in range(SEC):
+                        hit = sec == s + side
+                        for comp in range(2):
+                            r = (s * 2 + comp) * 8
+                            total[comp] = jnp.where(hit, got[r : r + 8, at], total[comp])
+                    for comp in range(2):
+                        value = jnp.sum(jnp.where(sub8 == within, total[comp], 0.0), axis=0, keepdims=True)
+                        r = rowpos(side, comp, i)
+                        tin[r : r + 1] = value
+
+    def exchange(par):
+        turned = tin[...].T
+        for comp in range(2):
+            msg[:, comp, :] = turned[comp * TILES : (comp + 1) * TILES] + G[comp : comp + 1]
+        send_rows(par)
+
+    node_tables(0, mine)
+    tin[...] = jnp.zeros_like(tin)
+    gather(0)
+    pull_tables(0, mine)
     cos_k = (lane8 - GROW) & 7
     col128 = iota((128, 128), 0)
     k128 = (iota((128, 128), 1) - GROW) & 7
@@ -261,6 +313,18 @@
                 if dr or dc:
                     yield row if dc == 0 else pltpu.roll(row, 1 if dc < 0 else 127, 1)
 
+    def turn_rows(par):
+        both = jnp.concatenate([box[par, :, 0, :], box[par, :, 1, :]], axis=0)
+        return both, both.T
+
+    wait_rows(0)
+    _, theirs = turn_rows(0)
+    yours = [theirs[16 * v : 16 * v + 16] for v in range(7)]
+    node_tables(1, yours)
+    gather(1)
+    G[...] = jnp.zeros_like(G)
+    exchange(1)
+    pull_tables(1, yours)
     for copy in kcopies:
         copy.wait()
     has_low, has_high = jnp.where(t > 0, 1.0, 0.0), jnp.where(t < TILES - 1, 1.0, 0.0)
@@ -276,48 +340,10 @@
             total = total + w
         WS[s] = total
 
-    def turn_rows(par):
-        both = jnp.concatenate([box[par, :, 0, :], box[par, :, 1, :]], axis=0)
-        return both, both.T
-
-    wait_rows(0)
-    _, theirs = turn_rows(0)
-    side_tables(1, [theirs[16 * v : 16 * v + 16] for v in range(7)])
-    tin[...] = jnp.zeros_like(tin)
-    G[...] = jnp.zeros_like(G)
     wrow[...] = jnp.zeros_like(wrow)
 
     ramp8 = 1.0 + (own_row0 + sub8).astype(F32) * (2.0 / 512)
     lens_step = LENS_RATE * SEC / (1024 * TILES)
-
-    def gather():
-        d_hi, d_lo = split(D[...].reshape(EXT * 16, 128))
-        both = jnp.concatenate([d_hi, d_lo], axis=1).astype(BF16)
-        for side in range(2):
-            for n in range(HALF // 2):
-                hot = CH[side, :, n * 256 : (n + 1) * 256]
-                got = jnp.dot(both, jnp.concatenate([hot, hot], axis=0), preferred_element_type=F32)
-                for m in range(2):
-                    i = 2 * n + m
-                    row = rowix[side, 0, i : i + 1]
-                    sec, within = lax.shift_right_logical(row, 3), row & 7
-                    at = slice(m * 128, (m + 1) * 128)
-                    total = [jnp.zeros((8, 128), F32), jnp.zeros((8, 128), F32)]
-                    for s in range(EXT):
-                        hit = sec == s
-                        for comp in range(2):
-                            r = (s * 2 + comp) * 8
-                            total[comp] = jnp.where(hit, got[r : r + 8, at], total[comp])
-                    for comp in range(2):
-                        value = jnp.sum(jnp.where(sub8 == within, total[comp], 0.0), axis=0, keepdims=True)
-                        r = rowpos(side, comp, i)
-                        tin[r : r + 1] = value
-
-    def exchange(par):
-        turned = tin[...].T
-        for comp in range(2):
-            msg[:, comp, :] = turned[comp * TILES : (comp + 1) * TILES] + G[comp : comp + 1]
-        send_rows(par)
 
     def take_gradient(both):
         for comp in range(2):
@@ -361,14 +387,15 @@
             pull[b : b + 24] = -base[b : b + 24] * r[b : b + 24] / (1.0 + size * 0.25)
 
     def scatter():
-        rows72 = iota((EXT * 8, 128), 0)
-        total = jnp.zeros((4 * EXT * 8, 128), F32)
+        rows = iota((SEC * 8, 128), 0)
+        got = []
         for side in range(2):
+            total = jnp.zeros((4 * SEC * 8, 128), F32)
             for n in range(HALF // 2):
                 cols = []
                 for m in range(2):
                     i = 2 * n + m
-                    hit = rows72 == rowix[side, 0, i : i + 1]
+                    hit = rows == rowix[side, 0, i : i + 1] - 8 * side
                     pieces = []
                     for comp in range(2):
                         r = rowpos(side, comp, i)
@@ -379,9 +406,12 @@
                     spread, CH[side, :, n * 256 : (n + 1) * 256], (((1,), (1,)), ((), ())),
                     preferred_element_type=F32,
                 )
+            total = total.reshape(2, 2, SEC, 8, 128)
+            got.append(total[:, 0] + total[:, 1])
         for comp in range(2):
-            b = comp * 2 * EXT * 8
-            F[:, comp] = (total[b : b + EXT * 8] + total[b + EXT * 8 : b + 2 * EXT * 8]).reshape(EXT, 8, 128)
+            F[0, comp] = got[0][comp, 0]
+            F[1:SEC, comp] = got[0][comp, 1:SEC] + got[1][comp, 0 : SEC - 1]
+            F[SEC, comp] = got[1][comp, SEC - 1]
 
     def springs(par):
         for s in range(EXT):
@@ -412,8 +442,6 @@
     def sweep(it, carry):
         par = lax.rem(it + 1, 2)
         hpar = lax.rem(it, 2)
-        gather()
-        exchange(par)
         for copy in beside(hpar):
             copy.wait()
         springs(hpar)
@@ -437,6 +465,13 @@
         F[SEC] = F[SEC] + yr[hpar, 1]
         gradient()
         D[...] = D[...] + STEP_RATE * (S[...] + F[...])
+
+        @pl.when(it < ITERS - 1)
+        def _():
+            gather(0)
+            gather(1)
+
+        exchange(1 - par)
         send_beside(1 - hpar)
         return carry
 
@@ -449,7 +484,6 @@
     lax.fori_loop(0, ITERS, sweep, 0)
     dout[...] = D[0:SEC]
     last = (ITERS + 1) % 2
-    exchange(last)
     for copy in beside(ITERS % 2):
         copy.wait()
     wait_rows(last)
@@ -462,10 +496,15 @@
 
 def on_device(displacement, lens_coef, stiff_class, stiff_table, match_src, match_owner, match_dst, match_level, match_offset):
     vmem = pl.BlockSpec(memory_space=pltpu.VMEM)
-    smem = pl.BlockSpec(memory_space=pltpu.SMEM)
+    hbm = pl.BlockSpec(memory_space=pltpu.HBM)
     V, DMA = pltpu.VMEM, pltpu.SemaphoreType.DMA
     lists = [a.reshape(8, 128) for a in (match_src, match_owner, match_dst, match_level)]
     scratch = [
+        V((SEC, 2, LENS), F32),
+        V((SEC, 8, 128), I32),
+        pltpu.SMEM((4,), F32),
+        V((8, 128), I32), V((8, 128), I32), V((8, 128), I32), V((8, 128), I32),
+        V((2, 1024), F32),
         V((EXT, 2, 8, 128), F32),
         V((EXT, 8, 128), F32),
         V((8, EXT, 8, 128), F32),
@@ -477,7 +516,6 @@
         V((2, 128, HALF * 128), BF16),
         V((2, 48, HALF * 128), BF16),
         V((2, 2, 16, 128), I32),
-        V((48, 128), F32),
         V((48, 128), F32),
         V((48, 128), F32),
         V((128, 128), F32),
@@ -494,7 +532,7 @@
         V((2, 2, 2, 8, 128), F32),
         V((2, 2, 2, 8, 128), F32),
         V((8, 128), F32),
-        DMA, DMA((2,)), DMA((2, 2)), DMA((2, 2)), DMA((2,)), DMA((2,)), DMA((2, 2)), DMA((2, 2)), DMA((3,)), DMA((3,)),
+        DMA((9,)), DMA, DMA((2,)), DMA((2, 2)), DMA((2, 2)), DMA((2,)), DMA((2,)), DMA((2, 2)), DMA((2, 2)), DMA((3,)), DMA((3,)),
     ]
     return pl.pallas_call(
         kernel,
@@ -502,11 +540,11 @@
             jax.ShapeDtypeStruct((SEC, 2, 8, 128), F32),
             jax.ShapeDtypeStruct((SEC, 2, LENS), F32),
         ),
-        in_specs=[vmem, vmem, vmem, smem] + [vmem] * 5,
+        in_specs=[hbm] * 9,
         out_specs=(vmem, vmem),
         scratch_shapes=scratch,
         compiler_params=pltpu.CompilerParams(
-            collective_id=0, has_side_effects=True, vmem_limit_bytes=32 * 1024 * 1024
+            collective_id=0, has_side_effects=True
         ),
         name="relax",
     )(displacement, lens_coef, stiff_class, stiff_table, *lists, match_offset)

time: 76.2 us -> 70.2 us (0.921)
  local copies, waits for them, and re-layouts: 6.95 us -> 2.08 us
  Pallas kernels: 68.2 us -> 67.3 us
    unnamed x20 -> x4, local copies, waits for them, and re-layouts: 6.95 us -> 2.08 us
    pallas_call x1, Pallas kernels: 68.2 us -> 67.3 us  [on_device(): pl.pallas_call(kernel, out_shape=(jax.ShapeDtypeStruct((SEC, 2, 8, 128),...]
where the time goes in v1:
time: 70.2 us; the launch traced here: 70.1 us
  Pallas kernels  67.3 us (96%)
  local copies, waits for them, and re-layouts  2.08 us (3%)
    pallas_call x1, Pallas kernels, on_device(): pl.pallas_call(kernel, out_shape=(jax.ShapeDtypeStruct((SEC, 2, 8, 128),...  67.3 us
    unnamed x4, local copies, waits for them, and re-layouts  2.08 us

profile of v1, /device:TPU:1, one launch (start us, length us, event | category | flops | bytes accessed | tf_op | source)
XLA Modules:
  0.0 70.1 jit_solution(7948250497329219994)
XLA Ops:
  0.6 67.3 %relax.1 = (f32[8,2,8,128]{3,2,1,0:T(8,128)}, f32[8,2,8]{2,1,0:T(2,128)}) custom-call(f32[8,2,8,128]{3,2,1,0:T(8,128)} %disp_in.1, f32[8,2,8]{2,1,0:T(2,128)} %lens_in.1, s32[8,8,128]{2,1,0:T(8,128)} %scls_in.1, f32[4]{0:T(128)} %stab_in.1, s32[8,128]{1,0:T(8,128)} %bitcast.4, s32[8,128]{1,0:T(8,128)} %bitcast.5, s32[8,128]{1,0:T(8,128)} %bitcast.6, ...), custom_call_target="tpu_custom_call" | custom-call | tf_op jit(solution)/shard_map/relax/pallas_call | solution.py:537
  68.0 0.0 copy-start
  68.0 1.5 %copy.13 = f32[8,2,8,128]{3,2,1,0:T(8,128)} copy(f32[8,2,8,128]{3,2,1,0:T(8,128)} %get-tuple-element.4) | data formatting | bytes 131072
  69.5 0.0 copy-done
  69.5 0.6 copy.14
Async XLA Ops:
  68.0 1.5 %copy-start = (f32[8,2,8]{2,1,0:T(2,128)S(1)}, f32[8,2,8]{2,1,0:T(2,128)}, u32[]{:S(2)}) copy-start(f32[8,2,8]{2,1,0:T(2,128)} %get-tuple-element.5) | copy-start | bytes 1540

commit v2 on v1

--- a/solution.py
+++ b/solution.py
@@ -43,6 +43,16 @@
     return x
 
 
+def along_lanes(source, lanes):
+    dims = lax.GatherDimensionNumbers(
+        offset_dims=(), collapsed_slice_dims=(1,), start_index_map=(1,),
+        operand_batching_dims=(0,), start_indices_batching_dims=(0,),
+    )
+    return lax.gather(
+        source, lanes[:, :, None], dims, slice_sizes=(1, 1), mode=lax.GatherScatterMode.PROMISE_IN_BOUNDS
+    )
+
+
 def pack_rows(a, b):
     last = jnp.where(iota((8, 128), 0) < 4, a[8:16], pltpu.roll(b[8:16], 4, 0))
     return jnp.concatenate([a[0:8], b[0:8], last], axis=0)
@@ -52,9 +62,9 @@
     disp_in, lens_in, scls_in, stab_in, msrc_in, mown_in, mdst_in, mlev_in, moff_in,
     dout, cout,
     lens, scls, stab, msrc, mown, mdst, mlev, moff,
-    D, K, W, WS, S, F, msg, box, CH, Q, rowix, offs, base, tin, pull, lval, C, G, tmp, wrow,
+    D, K, W, WS, S, F, msg, box, gmsg, ebox, CH, COS, L, rowix, slotix, ramps, offs, base, tin, pull, lval, C, G, tmp, wrow,
     hs, hr, khs, khr, ys, yr, cy,
-    in_sem, a_send, a_recv, h_send, h_recv, k_send, k_recv, y_send, y_recv, s_send, s_recv,
+    in_sem, a_send, a_recv, h_send, h_recv, k_send, k_recv, y_send, y_recv, s_send, s_recv, e_send, e_recv,
 ):
     t = lax.axis_index("tile")
     g = lax.axis_index("stack")
@@ -202,15 +212,18 @@
     def node_tables(side, values):
         sr, sc, dr, dc = [v.astype(I32) for v in values[0:4]]
         sec = lax.shift_right_logical(sr, 3)
-        rowix[side, 0] = sr if side == 0 else sec * 8 + 8 + dr
-        rowix[side, 1] = sec
+        own_row = sr if side == 0 else sec * 8 + 8 + dr
         own_col = sc if side == 0 else dc
+        rowix[side] = own_row
+        at = slice(24 * side, 24 * side + 24)
+        for n, v in enumerate((own_row, own_col, sec, sc, dc)):
+            slotix[n, at] = pack_rows(v, v)
         for i in range(HALF):
             at = slice(i * 128, (i + 1) * 128)
             CH[side, :, at] = jnp.where(iota((128, 128), 0) == own_col[i : i + 1], 1.0, 0.0).astype(BF16)
 
     def pull_tables(side, values):
-        sr, sc, dr, dc = [v.astype(I32) for v in values[0:4]]
+        sr, dr = values[0].astype(I32), values[2].astype(I32)
         ox, oy = values[5], values[6]
         sign = 1.0 if side == 0 else -1.0
         s_in = sr & 7
@@ -218,40 +231,49 @@
         ydst = (peer_row if side == 0 else own_row0) + dr
         ramp_s = (1.0 + ysrc.astype(F32) * (2.0 / 512)) * sign
         ramp_d = (1.0 + ydst.astype(F32) * (2.0 / 512)) * -sign
-        offs[24 * side : 24 * side + 24] = pack_rows(ox, oy) * sign
         weight = values[4] * 0.125
-        base[24 * side : 24 * side + 24] = pack_rows(weight, weight)
-        for i in range(HALF):
-            at = slice(i * 128, (i + 1) * 128)
-            parts = []
-            for col, ramp in ((sc, ramp_s), (dc, ramp_d)):
-                turn = (sub8 * col[i : i + 1]) & 255
-                high, low = split(jnp.cos(turn.astype(F32) * (np.pi / 128)) * ramp[i : i + 1])
-                parts += [high, high, low]
-            Q[side, :, at] = jnp.concatenate(parts, axis=0).astype(BF16)
-
-    def gather(side):
-        d_hi, d_lo = split(D[side : side + SEC].reshape(SEC * 16, 128))
+        at = slice(24 * side, 24 * side + 24)
+        offs[at] = pack_rows(ox, oy) * sign
+        base[at] = pack_rows(weight, weight)
+        ramps[0, at] = pack_rows(ramp_s, ramp_s)
+        ramps[1, at] = pack_rows(ramp_d, ramp_d)
+
+    def gather(side, first, count):
+        d_hi, d_lo = split(D[first : first + count].reshape(count * 16, 128))
         both = jnp.concatenate([d_hi, d_lo], axis=1).astype(BF16)
-        for _ in range(1):
-            for n in range(HALF // 2):
-                hot = CH[side, :, n * 256 : (n + 1) * 256]
-                got = jnp.dot(both, jnp.concatenate([hot, hot], axis=0), preferred_element_type=F32)
-                for m in range(2):
-                    i = 2 * n + m
-                    row = rowix[side, 0, i : i + 1]
-                    sec, within = lax.shift_right_logical(row, 3), row & 7
-                    at = slice(m * 128, (m + 1) * 128)
-                    total = [jnp.zeros((8, 128), F32), jnp.zeros((8, 128), F32)]
-                    for s in range(SEC):
-                        hit = sec == s + side
-                        for comp in range(2):
-                            r = (s * 2 + comp) * 8
-                            total[comp] = jnp.where(hit, got[r : r + 8, at], total[comp])
+        for n in range(HALF // 2):
+            hot = CH[side, :, n * 256 : (n + 1) * 256]
+            got = jnp.dot(both, jnp.concatenate([hot, hot], axis=0), preferred_element_type=F32)
+            for m in range(2):
+                i = 2 * n + m
+                row = rowix[side, i : i + 1]
+                sec, within = lax.shift_right_logical(row, 3), row & 7
+                at = slice(m * 128, (m + 1) * 128)
+                total = [jnp.zeros((8, 128), F32), jnp.zeros((8, 128), F32)]
+                for s in range(count):
+                    hit = sec == s + first
                     for comp in range(2):
-                        value = jnp.sum(jnp.where(sub8 == within, total[comp], 0.0), axis=0, keepdims=True)
-                        r = rowpos(side, comp, i)
-                        tin[r : r + 1] = value
+                        r = (s * 2 + comp) * 8
+                        total[comp] = jnp.where(hit, got[r : r + 8, at], total[comp])
+                for comp in range(2):
+                    value = jnp.sum(jnp.where(sub8 == within, total[comp], 0.0), axis=0, keepdims=True)
+                    r = rowpos(side, comp, i)
+                    tin[r : r + 1] = value
+
+    def by_comp(rows):
+        wide = [jnp.broadcast_to(row, (8, 128)) for row in rows]
+        return wide + [jnp.where(sub8 < 4, wide[0], wide[1])]
+
+    def gather_edge(side):
+        edge = side * SEC
+        blocks = [slice(24 * side + 8 * q, 24 * side + 8 * q + 8) for q in range(3)]
+        total = [jnp.zeros((8, 128), F32)] * 3
+        for r in range(8):
+            for q, source in enumerate(by_comp([D[edge, comp, r : r + 1] for comp in range(2)])):
+                found = along_lanes(source, slotix[1, blocks[q]])
+                total[q] = jnp.where(slotix[0, blocks[q]] == edge * 8 + r, found, total[q])
+        for q in range(3):
+            tin[blocks[q]] = tin[blocks[q]] + total[q]
 
     def exchange(par):
         turned = tin[...].T
@@ -261,14 +283,15 @@
 
     node_tables(0, mine)
     tin[...] = jnp.zeros_like(tin)
-    gather(0)
+    gather(0, 0, SEC)
     pull_tables(0, mine)
-    cos_k = (lane8 - GROW) & 7
-    col128 = iota((128, 128), 0)
-    k128 = (iota((128, 128), 1) - GROW) & 7
-    turn = (col128 * k128) & 255
-    cos_hi, cos_lo = split(jnp.cos(turn.astype(F32) * (np.pi / 128)))
-    cos_cat = jnp.concatenate([cos_hi, cos_hi, cos_lo], axis=0).astype(BF16)
+    for n in range(2):
+        k = (iota((128, 128), 1 - n) - GROW) & 7
+        turn = (iota((128, 128), n) * k) & 255
+        high, low = split(jnp.cos(turn.astype(F32) * (np.pi / 128)))
+        COS[n] = jnp.concatenate([high, high, low], axis=0).astype(BF16)
+    group16 = lax.shift_right_logical(iota((16, 128), 1), 3) - GROW // 8
+    mask16 = (group16 == iota((16, 128), 0)) & (group16 < EXT)
 
     for copy in first:
         copy.wait()
@@ -321,7 +344,7 @@
     _, theirs = turn_rows(0)
     yours = [theirs[16 * v : 16 * v + 16] for v in range(7)]
     node_tables(1, yours)
-    gather(1)
+    gather(1, 1, SEC)
     G[...] = jnp.zeros_like(G)
     exchange(1)
     pull_tables(1, yours)
@@ -353,26 +376,22 @@
     def lens_values():
         rows = []
         for comp in range(2):
-            wide = jnp.broadcast_to(C[comp : comp + 1], (8, 128))
-            s_hi, s_lo = split(fold(jnp.where(own_group, wide, 0.0)))
-            d_hi, d_lo = split(fold(jnp.where(group8 == sub8 + 1, wide, 0.0)))
-            block = lax.shift_right_logical(lane8, 3)
-            row = jnp.where(block == 1, s_lo, s_hi)
-            row = jnp.where(block >= 3, d_hi, row)
-            rows.append(jnp.where(block == 4, d_lo, row))
-        coef = jnp.concatenate(rows, axis=0)[:, 0:48].astype(BF16)
-        for side in range(2):
-            for n in range(HALF // 2):
-                got = jnp.dot(coef, Q[side, :, n * 256 : (n + 1) * 256], preferred_element_type=F32)
-                for m in range(2):
-                    i = 2 * n + m
-                    hit = rowix[side, 1, i : i + 1] == sub8
-                    for comp in range(2):
-                        r = rowpos(side, comp, i)
-                        lval[r : r + 1] = jnp.sum(
-                            jnp.where(hit, got[comp * 8 : comp * 8 + 8, m * 128 : (m + 1) * 128], 0.0),
-                            axis=0, keepdims=True,
-                        )
+            wide = jnp.broadcast_to(C[comp : comp + 1], (16, 128))
+            rows.append(jnp.where(mask16, wide, 0.0))
+        c_hi, c_lo = split(jnp.concatenate(rows, axis=0))
+        cat = jnp.concatenate([c_hi, c_lo, c_hi], axis=1).astype(BF16)
+        L[...] = jnp.dot(cat, COS[1], preferred_element_type=F32).reshape(2, 16, 128)
+        sources = [by_comp([L[comp, s : s + 1] for comp in range(2)]) for s in range(EXT)]
+        for b in range(6):
+            at = slice(8 * b, 8 * b + 8)
+            q = b % 3
+            sec = slotix[2, at]
+            own_end, far_end = jnp.zeros((8, 128), F32), jnp.zeros((8, 128), F32)
+            for s in range(SEC):
+                hit = sec == s
+                own_end = jnp.where(hit, along_lanes(sources[s][q], slotix[3, at]), own_end)
+                far_end = jnp.where(hit, along_lanes(sources[s + 1][q], slotix[4, at]), far_end)
+            lval[at] = ramps[0, at] * own_end + ramps[1, at] * far_end
 
     def forces(theirs):
         other = jnp.concatenate([theirs[24:48], theirs[0:24]], axis=0)
@@ -386,32 +405,26 @@
             size = jnp.concatenate([near, near, last], axis=0)
             pull[b : b + 24] = -base[b : b + 24] * r[b : b + 24] / (1.0 + size * 0.25)
 
-    def scatter():
-        rows = iota((SEC * 8, 128), 0)
-        got = []
-        for side in range(2):
-            total = jnp.zeros((4 * SEC * 8, 128), F32)
-            for n in range(HALF // 2):
-                cols = []
-                for m in range(2):
-                    i = 2 * n + m
-                    hit = rows == rowix[side, 0, i : i + 1] - 8 * side
-                    pieces = []
-                    for comp in range(2):
-                        r = rowpos(side, comp, i)
-                        pieces += list(split(pull[r : r + 1]))
-                    cols.append(jnp.concatenate([jnp.where(hit, p, 0.0) for p in pieces], axis=0))
-                spread = jnp.concatenate(cols, axis=1).astype(BF16)
-                total = total + lax.dot_general(
-                    spread, CH[side, :, n * 256 : (n + 1) * 256], (((1,), (1,)), ((), ())),
-                    preferred_element_type=F32,
-                )
-            total = total.reshape(2, 2, SEC, 8, 128)
-            got.append(total[:, 0] + total[:, 1])
-        for comp in range(2):
-            F[0, comp] = got[0][comp, 0]
-            F[1:SEC, comp] = got[0][comp, 1:SEC] + got[1][comp, 0 : SEC - 1]
-            F[SEC, comp] = got[1][comp, SEC - 1]
+    def scatter(side, first, count):
+        rows = iota((count * 8, 128), 0) + first * 8
+        total = jnp.zeros((4 * count * 8, 128), F32)
+        for n in range(HALF // 2):
+            cols = []
+            for m in range(2):
+                i = 2 * n + m
+                hit = rows == rowix[side, i : i + 1]
+                pieces = []
+                for comp in range(2):
+                    r = rowpos(side, comp, i)
+                    pieces += list(split(pull[r : r + 1]))
+                cols.append(jnp.concatenate([jnp.where(hit, p, 0.0) for p in pieces], axis=0))
+            spread = jnp.concatenate(cols, axis=1).astype(BF16)
+            total = total + lax.dot_general(
+                spread, CH[side, :, n * 256 : (n + 1) * 256], (((1,), (1,)), ((), ())),
+                preferred_element_type=F32,
+            )
+        total = total.reshape(2, 2, count, 8, 128)
+        return [total[comp, 0] + total[comp, 1] for comp in range(2)]
 
     def springs(par):
         for s in range(EXT):
@@ -424,22 +437,22 @@
                     total = total + W[n, s] * other
                 S[s, comp] = total
 
-    def gradient():
-        for s in range(EXT):
+    def ramp_sums(sections):
+        for s in sections:
             for comp in range(2):
                 r = comp * 16 + s
                 wrow[r : r + 1] = jnp.sum(ramp8 * F[s, comp], axis=0, keepdims=True)
+
+    def gradient():
         w_hi, w_lo = split(wrow[...])
         cat = jnp.concatenate([w_hi, w_lo, w_hi], axis=1).astype(BF16)
-        out = jnp.dot(cat, cos_cat, preferred_element_type=F32)
-        group16 = lax.shift_right_logical(iota((16, 128), 1), 3) - GROW // 8
-        mask = (group16 == iota((16, 128), 0)) & (group16 < EXT)
+        out = jnp.dot(cat, COS[0], preferred_element_type=F32)
         for comp in range(2):
             G[comp : comp + 1] = jnp.sum(
-                jnp.where(mask, out[comp * 16 : comp * 16 + 16], 0.0), axis=0, keepdims=True
+                jnp.where(mask16, out[comp * 16 : comp * 16 + 16], 0.0), axis=0, keepdims=True
             )
 
-    def sweep(it, carry):
+    def arrive(it):
         par = lax.rem(it + 1, 2)
         hpar = lax.rem(it, 2)
         for copy in beside(hpar):
@@ -450,45 +463,90 @@
         take_gradient(both)
         lens_values()
         forces(theirs)
-        scatter()
-        ys[hpar, 0] = F[SEC]
-        ys[hpar, 1] = F[0]
-        copies = [
-            t_like(hpar, 0, up_g),
-            t_like(hpar, 1, down_g),
-        ]
+        for side, edge in ((1, SEC), (0, 0)):
+            on_edge = scatter(side, edge, 1)
+            for comp in range(2):
+                F[edge, comp] = on_edge[comp][0]
+            ys[hpar, 1 - side] = F[edge]
+        copies = [y_pair(hpar, 0, up_g), y_pair(hpar, 1, down_g)]
         for copy in copies:
             copy.start()
+        return par, hpar, copies
+
+    def inner_forces():
+        inner = [scatter(side, 1, SEC - 1) for side in range(2)]
+        for comp in range(2):
+            F[1:SEC, comp] = inner[0][comp] + inner[1][comp]
+        ramp_sums(range(1, SEC))
+
+    def sweep(it, carry):
+        par, hpar, copies = arrive(it)
+        inner_forces()
+        D[1:SEC] = D[1:SEC] + STEP_RATE * (S[1:SEC] + F[1:SEC])
+        gather(0, 1, SEC - 1)
+        gather(1, 1, SEC - 1)
         for copy in copies:
             copy.wait()
-        F[0] = F[0] + yr[hpar, 0]
-        F[SEC] = F[SEC] + yr[hpar, 1]
+        for way, edge in ((0, 0), (1, SEC)):
+            F[edge] = F[edge] + yr[hpar, way]
+            D[edge] = D[edge] + STEP_RATE * (S[edge] + F[edge])
+        ramp_sums((0, SEC))
         gradient()
-        D[...] = D[...] + STEP_RATE * (S[...] + F[...])
-
-        @pl.when(it < ITERS - 1)
-        def _():
-            gather(0)
-            gather(1)
-
+
+        gather_edge(0)
+        gather_edge(1)
         exchange(1 - par)
         send_beside(1 - hpar)
         return carry
 
-    def t_like(par, way, other):
+    def y_pair(par, way, other):
         return pltpu.make_async_remote_copy(
             src_ref=ys.at[par, way], dst_ref=yr.at[par, way], send_sem=y_send.at[par, way],
             recv_sem=y_recv.at[par, way], device_id={"stack": other}, device_id_type=MESH,
         )
 
-    lax.fori_loop(0, ITERS, sweep, 0)
-    dout[...] = D[0:SEC]
-    last = (ITERS + 1) % 2
-    for copy in beside(ITERS % 2):
+    lax.fori_loop(0, ITERS - 1, sweep, 0)
+
+    last, lpar, copies = arrive(ITERS - 1)
+    inner_forces()
+    ramp_sums((0, SEC))
+    gradient()
+    gmsg[...] = G[0:2]
+    fin = 1 - last
+
+    def send_gradient(p):
+        pltpu.make_async_remote_copy(
+            src_ref=gmsg, dst_ref=box.at[fin, t], send_sem=a_send, recv_sem=a_recv.at[fin],
+            device_id={"tile": p}, device_id_type=MESH,
+        ).start()
+
+    def send_edge(p):
+        pltpu.make_async_remote_copy(
+            src_ref=gmsg, dst_ref=ebox.at[t], send_sem=e_send, recv_sem=e_recv,
+            device_id={"stack": up_g, "tile": p}, device_id_type=MESH,
+        ).start()
+
+    def send_both(p):
+        send_edge(p)
+        send_gradient(p)
+
+    each_peer(send_both)
+    send_edge(t)
+    box[fin, t] = gmsg[...]
+    for copy in copies:
         copy.wait()
-    wait_rows(last)
-    both = jnp.concatenate([box[last, :, 0, :], box[last, :, 1, :]], axis=0)
-    take_gradient(both)
+    F[0] = F[0] + yr[lpar, 0]
+    dout[...] = D[0:SEC] + STEP_RATE * (S[0:SEC] + F[0:SEC])
+    wait_rows(fin)
+    pltpu.make_async_copy(ebox, ebox, e_recv).wait()
+    pltpu.make_async_copy(ebox, ebox, e_send).wait()
+    for comp in range(2):
+        total = jnp.sum(box[fin, :, comp, :], axis=0, keepdims=True)
+        below = jnp.sum(ebox[:, comp, :], axis=0, keepdims=True)
+        below = pltpu.roll(below, 128 - LENS * SEC, 1)
+        first = jnp.where(group8[0:1] == 0, below, 0.0)
+        total = jnp.where((group8[0:1] >= 0) & (group8[0:1] < SEC), total + first, 0.0)
+        C[comp : comp + 1] = C[comp : comp + 1] + lens_step * total
     for comp in range(2):
         wide = fold(jnp.where(own_group, jnp.broadcast_to(C[comp : comp + 1], (8, 128)), 0.0))
         cout[:, comp, :] = wide[:, 0:LENS]
@@ -513,9 +571,14 @@
         V((EXT, 2, 8, 128), F32),
         V((TILES, 2, 128), F32),
         V((2, TILES, 2, 128), F32),
+        V((2, 128), F32),
+        V((TILES, 2, 128), F32),
         V((2, 128, HALF * 128), BF16),
-        V((2, 48, HALF * 128), BF16),
-        V((2, 2, 16, 128), I32),
+        V((2, 3 * 128, 128), BF16),
+        V((2, 16, 128), F32),
+        V((2, 16, 128), I32),
+        V((5, 48, 128), I32),
+        V((2, 48, 128), F32),
         V((48, 128), F32),
         V((48, 128), F32),
         V((128, 128), F32),
@@ -532,14 +595,15 @@
         V((2, 2, 2, 8, 128), F32),
         V((2, 2, 2, 8, 128), F32),
         V((8, 128), F32),
-        DMA((9,)), DMA, DMA((2,)), DMA((2, 2)), DMA((2, 2)), DMA((2,)), DMA((2,)), DMA((2, 2)), DMA((2, 2)), DMA((3,)), DMA((3,)),
+        DMA((9,)), DMA, DMA((2,)), DMA((2, 2)), DMA((2, 2)), DMA((2,)), DMA((2,)), DMA((2, 2)), DMA((2, 2)), DMA((3,)), DMA((3,)), DMA, DMA,
     ]
+    outs = (
+        jax.ShapeDtypeStruct((SEC, 2, 8, 128), F32),
+        jax.ShapeDtypeStruct((SEC, 2, LENS), F32),
+    )
     return pl.pallas_call(
         kernel,
-        out_shape=(
-            jax.ShapeDtypeStruct((SEC, 2, 8, 128), F32),
-            jax.ShapeDtypeStruct((SEC, 2, LENS), F32),
-        ),
+        out_shape=outs,
         in_specs=[hbm] * 9,
         out_specs=(vmem, vmem),
         scratch_shapes=scratch,

time: 70.2 us -> 67 us (0.954)
  Pallas kernels: 67.3 us -> 64.1 us
    pallas_call x1, Pallas kernels: 67.3 us -> 64.1 us  [on_device(): pl.pallas_call(kernel, out_shape=outs, in_specs=[hbm] * 9, out_specs=(vme...]
where the time goes in v2:
time: 67 us; the launch traced here: 66.8 us
  Pallas kernels  64.1 us (96%)
  local copies, waits for them, and re-layouts  2.08 us (3%)
    pallas_call x1, Pallas kernels, on_device(): pl.pallas_call(kernel, out_shape=outs, in_specs=[hbm] * 9, out_specs=(vme...  64.1 us
    unnamed x4, local copies, waits for them, and re-layouts  2.08 us

profile of v2, /device:TPU:1, one launch (start us, length us, event | category | flops | bytes accessed | tf_op | source)
XLA Modules:
  0.0 66.8 jit_solution(10984626640331036677)
XLA Ops:
  0.6 64.1 %relax.1 = (f32[8,2,8,128]{3,2,1,0:T(8,128)}, f32[8,2,8]{2,1,0:T(2,128)}) custom-call(f32[8,2,8,128]{3,2,1,0:T(8,128)} %disp_in.1, f32[8,2,8]{2,1,0:T(2,128)} %lens_in.1, s32[8,8,128]{2,1,0:T(8,128)} %scls_in.1, f32[4]{0:T(128)} %stab_in.1, s32[8,128]{1,0:T(8,128)} %bitcast.4, s32[8,128]{1,0:T(8,128)} %bitcast.5, s32[8,128]{1,0:T(8,128)} %bitcast.6, ...), custom_call_target="tpu_custom_call" | custom-call | tf_op jit(solution)/shard_map/relax/pallas_call | solution.py:604
  64.7 0.0 copy-start
  64.8 1.5 %copy.13 = f32[8,2,8,128]{3,2,1,0:T(8,128)} copy(f32[8,2,8,128]{3,2,1,0:T(8,128)} %get-tuple-element.4) | data formatting | bytes 131072
  66.2 0.0 copy-done
  66.2 0.6 copy.14
Async XLA Ops:
  64.7 1.5 %copy-start = (f32[8,2,8]{2,1,0:T(2,128)S(1)}, f32[8,2,8]{2,1,0:T(2,128)}, u32[]{:S(2)}) copy-start(f32[8,2,8]{2,1,0:T(2,128)} %get-tuple-element.5) | copy-start | bytes 1540

commit v3 on v2

--- a/solution.py
+++ b/solution.py
@@ -62,7 +62,7 @@
     disp_in, lens_in, scls_in, stab_in, msrc_in, mown_in, mdst_in, mlev_in, moff_in,
     dout, cout,
     lens, scls, stab, msrc, mown, mdst, mlev, moff,
-    D, K, W, WS, S, F, msg, box, gmsg, ebox, CH, COS, L, rowix, slotix, ramps, offs, base, tin, pull, lval, C, G, tmp, wrow,
+    D, K, W, WS, S, F, msg, box, gmsg, ebox, CH, CHT, COS, L, rowix, slotix, ramps, offs, base, tin, pull, lval, C, G, tmp, wrow,
     hs, hr, khs, khr, ys, yr, cy,
     in_sem, a_send, a_recv, h_send, h_recv, k_send, k_recv, y_send, y_recv, s_send, s_recv, e_send, e_recv,
 ):
@@ -237,6 +237,10 @@
         base[at] = pack_rows(weight, weight)
         ramps[0, at] = pack_rows(ramp_s, ramp_s)
         ramps[1, at] = pack_rows(ramp_d, ramp_d)
+        own_col = (values[1] if side == 0 else values[3]).astype(I32)
+        for i in range(HALF):
+            hot = jnp.where(iota((128, 128), 0) == own_col[i : i + 1], 1.0, 0.0)
+            CHT[side, i * 128 : (i + 1) * 128] = hot.T.astype(BF16)
 
     def gather(side, first, count):
         d_hi, d_lo = split(D[first : first + count].reshape(count * 16, 128))
@@ -277,8 +281,9 @@
 
     def exchange(par):
         turned = tin[...].T
+        flat = msg.reshape(128, 128)
         for comp in range(2):
-            msg[:, comp, :] = turned[comp * TILES : (comp + 1) * TILES] + G[comp : comp + 1]
+            flat[pl.ds(comp, TILES, stride=2), :] = turned[comp * TILES : (comp + 1) * TILES] + G[comp : comp + 1]
         send_rows(par)
 
     node_tables(0, mine)
@@ -337,7 +342,8 @@
                     yield row if dc == 0 else pltpu.roll(row, 1 if dc < 0 else 127, 1)
 
     def turn_rows(par):
-        both = jnp.concatenate([box[par, :, 0, :], box[par, :, 1, :]], axis=0)
+        flat = box.at[par].reshape(128, 128)
+        both = jnp.concatenate([flat[pl.ds(n, TILES, stride=2), :] for n in range(2)], axis=0)
         return both, both.T
 
     wait_rows(0)
@@ -419,9 +425,8 @@
                     pieces += list(split(pull[r : r + 1]))
                 cols.append(jnp.concatenate([jnp.where(hit, p, 0.0) for p in pieces], axis=0))
             spread = jnp.concatenate(cols, axis=1).astype(BF16)
-            total = total + lax.dot_general(
-                spread, CH[side, :, n * 256 : (n + 1) * 256], (((1,), (1,)), ((), ())),
-                preferred_element_type=F32,
+            total = total + jnp.dot(
+                spread, CHT[side, n * 256 : (n + 1) * 256], preferred_element_type=F32
             )
         total = total.reshape(2, 2, count, 8, 128)
         return [total[comp, 0] + total[comp, 1] for comp in range(2)]
@@ -574,6 +579,7 @@
         V((2, 128), F32),
         V((TILES, 2, 128), F32),
         V((2, 128, HALF * 128), BF16),
+        V((2, HALF * 128, 128), BF16),
         V((2, 3 * 128, 128), BF16),
         V((2, 16, 128), F32),
         V((2, 16, 128), I32),

time: 67 us -> 66.4 us (level)
  no operation moved by 1% of the time
where the time goes in v3:
time: 66.4 us; the launch traced here: 66.3 us
  Pallas kernels  63.5 us (96%)
  local copies, waits for them, and re-layouts  2.08 us (3%)
    pallas_call x1, Pallas kernels, on_device(): pl.pallas_call(kernel, out_shape=outs, in_specs=[hbm] * 9, out_specs=(vme...  63.5 us
    unnamed x4, local copies, waits for them, and re-layouts  2.08 us

profile of v3, /device:TPU:1, one launch (start us, length us, event | category | flops | bytes accessed | tf_op | source)
XLA Modules:
  0.0 66.3 jit_solution(9521664122175972397)
XLA Ops:
  0.6 63.5 %relax.1 = (f32[8,2,8,128]{3,2,1,0:T(8,128)}, f32[8,2,8]{2,1,0:T(2,128)}) custom-call(f32[8,2,8,128]{3,2,1,0:T(8,128)} %disp_in.1, f32[8,2,8]{2,1,0:T(2,128)} %lens_in.1, s32[8,8,128]{2,1,0:T(8,128)} %scls_in.1, f32[4]{0:T(128)} %stab_in.1, s32[8,128]{1,0:T(8,128)} %bitcast.4, s32[8,128]{1,0:T(8,128)} %bitcast.5, s32[8,128]{1,0:T(8,128)} %bitcast.6, ...), custom_call_target="tpu_custom_call" | custom-call | tf_op jit(solution)/shard_map/relax/pallas_call | solution.py:610
  64.2 0.0 copy-start
  64.2 1.5 %copy.13 = f32[8,2,8,128]{3,2,1,0:T(8,128)} copy(f32[8,2,8,128]{3,2,1,0:T(8,128)} %get-tuple-element.4) | data formatting | bytes 131072
  65.7 0.0 copy-done
  65.7 0.6 copy.14
Async XLA Ops:
  64.2 1.5 %copy-start = (f32[8,2,8]{2,1,0:T(2,128)S(1)}, f32[8,2,8]{2,1,0:T(2,128)}, u32[]{:S(2)}) copy-start(f32[8,2,8]{2,1,0:T(2,128)} %get-tuple-element.5) | copy-start | bytes 1540

commit v4 on v3

--- a/solution.py
+++ b/solution.py
@@ -62,7 +62,7 @@
     disp_in, lens_in, scls_in, stab_in, msrc_in, mown_in, mdst_in, mlev_in, moff_in,
     dout, cout,
     lens, scls, stab, msrc, mown, mdst, mlev, moff,
-    D, K, W, WS, S, F, msg, box, gmsg, ebox, CH, CHT, COS, L, rowix, slotix, ramps, offs, base, tin, pull, lval, C, G, tmp, wrow,
+    D, K, W, WS, S, F, msg, box, gmsg, ebox, CH, CHT, COS, L, rowix, slotix, basis, offs, base, tin, pull, lval, C, G, tmp, wrow,
     hs, hr, khs, khr, ys, yr, cy,
     in_sem, a_send, a_recv, h_send, h_recv, k_send, k_recv, y_send, y_recv, s_send, s_recv, e_send, e_recv,
 ):
@@ -235,8 +235,11 @@
         at = slice(24 * side, 24 * side + 24)
         offs[at] = pack_rows(ox, oy) * sign
         base[at] = pack_rows(weight, weight)
-        ramps[0, at] = pack_rows(ramp_s, ramp_s)
-        ramps[1, at] = pack_rows(ramp_d, ramp_d)
+        for end, ramp in ((0, ramp_s), (1, ramp_d)):
+            wide = pack_rows(ramp, ramp)
+            for k in range(LENS):
+                turn = (k * slotix[3 + end, at]) & 255
+                basis[end, k, at] = wide * jnp.cos(turn.astype(F32) * (np.pi / 128))
         own_col = (values[1] if side == 0 else values[3]).astype(I32)
         for i in range(HALF):
             hot = jnp.where(iota((128, 128), 0) == own_col[i : i + 1], 1.0, 0.0)
@@ -296,6 +299,7 @@
         high, low = split(jnp.cos(turn.astype(F32) * (np.pi / 128)))
         COS[n] = jnp.concatenate([high, high, low], axis=0).astype(BF16)
     group16 = lax.shift_right_logical(iota((16, 128), 1), 3) - GROW // 8
+    mask72 = iota((EXT * LENS, 128), 1) - GROW == iota((EXT * LENS, 128), 0)
     mask16 = (group16 == iota((16, 128), 0)) & (group16 < EXT)
 
     for copy in first:
@@ -382,22 +386,28 @@
     def lens_values():
         rows = []
         for comp in range(2):
-            wide = jnp.broadcast_to(C[comp : comp + 1], (16, 128))
-            rows.append(jnp.where(mask16, wide, 0.0))
+            wide = jnp.broadcast_to(C[comp : comp + 1], (EXT * LENS, 128))
+            rows.append(jnp.where(mask72, wide, 0.0))
         c_hi, c_lo = split(jnp.concatenate(rows, axis=0))
-        cat = jnp.concatenate([c_hi, c_lo, c_hi], axis=1).astype(BF16)
-        L[...] = jnp.dot(cat, COS[1], preferred_element_type=F32).reshape(2, 16, 128)
-        sources = [by_comp([L[comp, s : s + 1] for comp in range(2)]) for s in range(EXT)]
+        cat = jnp.concatenate([c_hi, c_lo], axis=1).astype(BF16)
+        ones = jnp.ones((256, 128), BF16)
+        L[...] = jnp.dot(cat, ones, preferred_element_type=F32).reshape(2, EXT * LENS, 128)
+        blocks = [slice(8 * b, 8 * b + 8) for b in range(6)]
+        hits = [[slotix[2, blocks[b]] == s for s in range(1, SEC)] for b in range(6)]
+        total = [jnp.zeros((8, 128), F32)] * 6
+        for end in range(2):
+            for k in range(LENS):
+                coefs = []
+                for s in range(SEC):
+                    at = (s + end) * LENS + k
+                    coefs.append(by_comp([L[comp, at : at + 1] for comp in range(2)]))
+                for b in range(6):
+                    coef = coefs[0][b % 3]
+                    for s in range(1, SEC):
+                        coef = jnp.where(hits[b][s - 1], coefs[s][b % 3], coef)
+                    total[b] = total[b] + coef * basis[end, k, blocks[b]]
         for b in range(6):
-            at = slice(8 * b, 8 * b + 8)
-            q = b % 3
-            sec = slotix[2, at]
-            own_end, far_end = jnp.zeros((8, 128), F32), jnp.zeros((8, 128), F32)
-            for s in range(SEC):
-                hit = sec == s
-                own_end = jnp.where(hit, along_lanes(sources[s][q], slotix[3, at]), own_end)
-                far_end = jnp.where(hit, along_lanes(sources[s + 1][q], slotix[4, at]), far_end)
-            lval[at] = ramps[0, at] * own_end + ramps[1, at] * far_end
+            lval[blocks[b]] = total[b]
 
     def forces(theirs):
         other = jnp.concatenate([theirs[24:48], theirs[0:24]], axis=0)
@@ -581,10 +591,10 @@
         V((2, 128, HALF * 128), BF16),
         V((2, HALF * 128, 128), BF16),
         V((2, 3 * 128, 128), BF16),
-        V((2, 16, 128), F32),
+        V((2, EXT * LENS, 128), F32),
         V((2, 16, 128), I32),
         V((5, 48, 128), I32),
-        V((2, 48, 128), F32),
+        V((2, LENS, 48, 128), F32),
         V((48, 128), F32),
         V((48, 128), F32),
         V((128, 128), F32),

time: 66.4 us -> 66 us (level)
  no operation moved by 1% of the time
where the time goes in v4:
time: 66 us; the launch traced here: 65.9 us
  Pallas kernels  63.1 us (96%)
  local copies, waits for them, and re-layouts  2.08 us (3%)
    pallas_call x1, Pallas kernels, on_device(): pl.pallas_call(kernel, out_shape=outs, in_specs=[hbm] * 9, out_specs=(vme...  63.1 us
    unnamed x4, local copies, waits for them, and re-layouts  2.08 us

profile of v4, /device:TPU:1, one launch (start us, length us, event | category | flops | bytes accessed | tf_op | source)
XLA Modules:
  0.0 65.9 jit_solution(9701250840553914607)
XLA Ops:
  0.6 63.1 %relax.1 = (f32[8,2,8,128]{3,2,1,0:T(8,128)}, f32[8,2,8]{2,1,0:T(2,128)}) custom-call(f32[8,2,8,128]{3,2,1,0:T(8,128)} %disp_in.1, f32[8,2,8]{2,1,0:T(2,128)} %lens_in.1, s32[8,8,128]{2,1,0:T(8,128)} %scls_in.1, f32[4]{0:T(128)} %stab_in.1, s32[8,128]{1,0:T(8,128)} %bitcast.4, s32[8,128]{1,0:T(8,128)} %bitcast.5, s32[8,128]{1,0:T(8,128)} %bitcast.6, ...), custom_call_target="tpu_custom_call" | custom-call | tf_op jit(solution)/shard_map/relax/pallas_call | solution.py:620
  63.8 0.0 copy-start
  63.8 1.5 %copy.13 = f32[8,2,8,128]{3,2,1,0:T(8,128)} copy(f32[8,2,8,128]{3,2,1,0:T(8,128)} %get-tuple-element.4) | data formatting | bytes 131072
  65.3 0.0 copy-done
  65.3 0.6 copy.14
Async XLA Ops:
  63.8 1.5 %copy-start = (f32[8,2,8]{2,1,0:T(2,128)S(1)}, f32[8,2,8]{2,1,0:T(2,128)}, u32[]{:S(2)}) copy-start(f32[8,2,8]{2,1,0:T(2,128)} %get-tuple-element.5) | copy-start | bytes 1540
